TPU v7x, 256 devices: a whole 4x4x8 slice. The times are simulated.
256 devices in a mesh: depth: 32 (over x, z_lo, y), cols: 8 (over z_hi, core).
Axes of the slice: x: 4, y: 4, z: 8 (z_hi: 4, z_lo: 2; z = z_hi * 2 + z_lo), core: 2. Of those that a mesh axis runs over, the one named last changes fastest.
Arguments:
- amplitudes: float32 [2304, 32768], P('cols', 'depth'), may hold values from -6 to 6
- integrals: float32 [32768, 8192], P('depth', 'cols'), may hold values from -0.03125 to 0.03125
- residual_in: float32 [2304, 8192], P('depth', 'cols'), may hold values from -4 to 4
Outputs:
- residual_out: float32 [2304, 8192], P('depth', 'cols')
All inputs are finite; a program needn't handle non-finite values.
Results may differ from a plain program's by a relative error of at most 0.000071.
Values sent between devices are 32-bit elements; how exact they have to be, the bound alone decides.
A program may use at most 64 MiB of HBM per device.

v0:
```python
import jax
import jax.numpy as jnp
from jax import lax
from jax.sharding import PartitionSpec as P


def shards(amplitudes, integrals, residual_in):
    panel = lax.all_gather(amplitudes, "cols", axis=0, tiled=True)
    partial_value = jnp.dot(
        panel, integrals, precision=lax.Precision.HIGHEST, preferred_element_type=jnp.float32
    )
    owned = lax.psum_scatter(partial_value, "depth", scatter_dimension=0, tiled=True)
    return residual_in + owned


def solution(mesh):
    placed = (P("cols", "depth"), P("depth", "cols"), P("depth", "cols"))
    return jax.shard_map(
        shards, mesh=mesh, in_specs=placed, out_specs=P("depth", "cols"), check_vma=False
    )
```

profile of v0, /device:TPU:64, one launch (start us, length us, event | category | flops | bytes accessed | tf_op | source)
XLA Modules:
  0.0 334.9 jit_solution(11174748517182940044)
XLA Ops:
  6.5 0.0 all-gather.2.cloned.1.call-start
  6.5 0.7 all-gather.2.cloned.1.call-update
  7.3 0.0 reduce-scatter.2.cloned.1.call-start
  7.3 100.3 %all-gather.2.cloned.1.call-done = f32[2304,1024]{1,0:T(8,128)} async-done(((f32[288,1024]{1,0:T(8,128)}), f32[2304,1024]{1,0:T(8,128)}) %all-gather.2.cloned.1.call-update) | async-done | bytes 9437200 | tf_op jit(solution)/shard_map/all_gather | solution.py:8
  107.6 35.3 %fusion = f32[2304,1024]{1,0:T(8,128)} fusion(f32[2304,1024]{1,0:T(8,128)} %all-gather.2.cloned.1.call-done, f32[1024,1024]{1,0:T(8,128)} %param.4), kind=kOutput, calls=%fused_computation | convolution fusion | flops 28991029248 | bytes 23068672 | tf_op jit(solution)/shard_map/dot_general | solution.py:9
  142.9 0.0 copy-start
  142.9 0.0 reduce-scatter.2.cloned.1.call-update
  142.9 183.5 %reduce-scatter.2.cloned.1.call-done = f32[72,1024]{1,0:T(8,128)} async-done(((f32[2304,1024]{1,0:T(8,128)}), f32[72,1024]{1,0:T(8,128)}) %reduce-scatter.2.cloned.1.call-update) | async-done | bytes 294928 | tf_op jit(solution)/shard_map/reduce_scatter | solution.py:12
  326.4 0.0 copy-done
  326.4 1.7 add.5
Async XLA Ops:
  6.5 101.1 %all-gather.2.cloned.1.call-start = ((), (), s32[]{:S(2)}) async-start(), calls=%async_computation.1 | async-start | bytes 10616832 | tf_op jit(solution)/shard_map/all_gather | solution.py:8
  7.3 319.1 %reduce-scatter.2.cloned.1.call-start = ((), (), s32[]{:S(2)}) async-start(), calls=%async_computation.2 | async-start | bytes 9732096 | tf_op jit(solution)/shard_map/reduce_scatter | solution.py:12
  142.9 183.5 %copy-start = (f32[72,1024]{1,0:T(8,128)S(1)}, f32[72,1024]{1,0:T(8,128)}, u32[]{:S(2)}) copy-start(f32[72,1024]{1,0:T(8,128)} %param.5) | copy-start | bytes 884740
Sparse Core Ops, SparseCore 0:
  9.2 98.3 all-gather.1
  143.0 183.2 reduce-scatter.1
where the time goes:
time: 335 us
  waiting for transfers between devices  284 us (85%)
  matrix products  35.3 us (11%)
  between operations  13.4 us (4%)
    reduce_scatter x1, waiting for transfers between devices, shards(): lax.psum_scatter(partial_value, 'depth', scatter_dimension=0, tiled=True)  183 us
    all_gather x1, waiting for transfers between devices, shards(): panel = lax.all_gather(amplitudes, 'cols', axis=0, tiled=True)  100 us
    dot_general x1, matrix products, shards(): jnp.dot(panel, integrals, precision=lax.Precision.HIGHEST, preferred_elem...  35.3 us
  transfers between devices with their start and end apart: 2, of which 2 were waited for; matrix products, arithmetic and copies ran while one was open for 0% of the time, Pallas kernels for 0%

commit v1 on v0

--- a/solution.py
+++ b/solution.py
@@ -5,7 +5,8 @@
 
 
 def shards(amplitudes, integrals, residual_in):
-    panel = lax.all_gather(amplitudes, "cols", axis=0, tiled=True)
+    sent = jnp.stack([amplitudes] * lax.axis_size("cols"))
+    panel = jnp.concatenate(lax.all_to_all(sent, "cols", 0, 0), axis=0)
     partial_value = jnp.dot(
         panel, integrals, precision=lax.Precision.HIGHEST, preferred_element_type=jnp.float32
     )

time: 335 us -> 451 us (1.35)
  blocking collectives: 0 us -> 214 us
  waiting for transfers between devices: 284 us -> 186 us
    all_to_all x0 -> x1, blocking collectives: none -> 214 us  [shards(): panel = jnp.concatenate(lax.all_to_all(sent, 'cols', 0, 0), axis=0)]
    all_gather x1 -> x0, waiting for transfers between devices: 100 us -> none  [shards(): panel = lax.all_gather(amplitudes, 'cols', axis=0, tiled=True)]
  transfers between devices with their start and end apart: 2 -> 1, of which waited for: 2 -> 1; matrix products, arithmetic and copies ran while one was open for 0% -> 0% of each run, Pallas kernels for 0% -> 0%
where the time goes in v1:
time: 451 us
  blocking collectives  214 us (47%)
  waiting for transfers between devices  186 us (41%)
  matrix products  32.5 us (7%)
  between operations  13.4 us (3%)
    all_to_all x1, blocking collectives, shards(): panel = jnp.concatenate(lax.all_to_all(sent, 'cols', 0, 0), axis=0)  214 us
    reduce_scatter x1, waiting for transfers between devices, shards(): lax.psum_scatter(partial_value, 'depth', scatter_dimension=0, tiled=True)  186 us
    dot_general x1, matrix products, shards(): jnp.dot(panel, integrals, precision=lax.Precision.HIGHEST, preferred_elem...  32.5 us
  transfers between devices with their start and end apart: 1, of which 1 were waited for; matrix products, arithmetic and copies ran while one was open for 0% of the time, Pallas kernels for 0%

profile of v1, /device:TPU:64, one launch (start us, length us, event | category | flops | bytes accessed | tf_op | source)
XLA Modules:
  0.0 450.7 jit_solution(5448672744346460753)
XLA Ops:
  6.5 0.0 reduce-scatter.2.cloned.1.call-start
  6.5 2.5 stack.2
  9.0 0.0 copy-start.1
  9.0 214.1 %all_to_all.5 = f32[8,288,1024]{2,1,0:T(8,128)S(1)} all-to-all(f32[8,288,1024]{2,1,0:T(8,128)S(1)} %stack.2), channel_id=1, replica_groups=mesh['depth'=32,'cols'=8] {'cols'}, dimensions={0} | all-to-all | bytes 18874368 | tf_op jit(solution)/shard_map/all_to_all | solution.py:9
  223.1 0.0 copy-done.1
  223.2 32.5 %fusion = f32[2304,1024]{1,0:T(8,128)} fusion(f32[2304,1024]{1,0:T(8,128)S(1)} %bitcast.3, f32[1024,1024]{1,0:T(8,128)S(1)} %copy-done.1), kind=kOutput, calls=%fused_computation | convolution fusion | flops 28991029248 | bytes 23068672 | tf_op jit(solution)/shard_map/dot_general | solution.py:10
  255.7 0.0 copy-start
  255.7 0.0 reduce-scatter.2.cloned.1.call-update
  255.7 186.4 %reduce-scatter.2.cloned.1.call-done = f32[72,1024]{1,0:T(8,128)} async-done(((f32[2304,1024]{1,0:T(8,128)}), f32[72,1024]{1,0:T(8,128)}) %reduce-scatter.2.cloned.1.call-update) | async-done | bytes 294928 | tf_op jit(solution)/shard_map/reduce_scatter | solution.py:13
  442.1 0.0 copy-done
  442.1 1.7 add.5
Async XLA Ops:
  6.5 435.6 %reduce-scatter.2.cloned.1.call-start = ((), (), s32[]{:S(2)}) async-start(), calls=%async_computation.2 | async-start | bytes 9732096 | tf_op jit(solution)/shard_map/reduce_scatter | solution.py:13
  9.0 214.2 %copy-start.1 = (f32[1024,1024]{1,0:T(8,128)S(1)}, f32[1024,1024]{1,0:T(8,128)}, u32[]{:S(2)}) copy-start(f32[1024,1024]{1,0:T(8,128)} %param.4) | copy-start | bytes 12582916
  255.7 186.4 %copy-start = (f32[72,1024]{1,0:T(8,128)S(1)}, f32[72,1024]{1,0:T(8,128)}, u32[]{:S(2)}) copy-start(f32[72,1024]{1,0:T(8,128)} %param.5) | copy-start | bytes 884740
Sparse Core Ops, SparseCore 0:
  255.8 186.2 reduce-scatter.1
